TPU v7x, 512 devices: a whole 4x8x8 slice. The times are simulated.
512 devices in a mesh: dp: 64 (over x, y_hi, z), tensor: 8 (over y_lo, core).
Axes of the slice: x: 4, y: 8 (y_hi: 2, y_lo: 4; y = y_hi * 4 + y_lo), z: 8, core: 2. Of those that a mesh axis runs over, the one named last changes fastest.
Arguments:
- frames_in: bfloat16 [64, 1024, 1536], P('dp', 'tensor'), may hold values from -6 to 6
- lengths: int32 [64], P('dp'), may hold values from 341 to 1024, as said below
- ln_gain: float32 [1536], replicated, may hold values from 0.5 to 2
- ln_bias: float32 [1536], replicated, may hold values from -3 to 3
- glu_weight: bfloat16 [2, 1536, 1536], P(None, 'tensor'), may hold values from -0.15625 to 0.15625
- conv_kernel: bfloat16 [32, 1536], P(None, 'tensor'), may hold values from -1 to 1
- bn_gain: float32 [1536], P('tensor'), may hold values from 0.5 to 2
- bn_bias: float32 [1536], P('tensor'), may hold values from -3 to 3
- out_weight: bfloat16 [1536, 1536], P('tensor'), may hold values from -0.15625 to 0.15625
Outputs:
- frames_out: bfloat16 [64, 1024, 1536], P('dp', 'tensor')
Inputs may be any that keep to these rules, and one draw needn't show every extreme that they name: `lengths`: each span's length lies between 341 and 1024; some span is full in every draw.
All inputs are finite; a program needn't handle non-finite values.
Results may differ from a plain program's by a relative error of at most 0.0095.
Values may be sent and summed in bfloat16 or wider, within the bound.
A program may use at most 64 MiB of HBM per device.

v0:
```python
import jax
import jax.numpy as jnp
from jax import lax
from jax.sharding import PartitionSpec as P

KERNEL = 32


def layer_norm(rows, gain, bias):
    values = rows.astype(jnp.float32)
    center = jnp.mean(values, axis=-1, keepdims=True)
    spread = jnp.mean((values - center) ** 2, axis=-1, keepdims=True)
    return ((values - center) * lax.rsqrt(spread + 1e-05) * gain + bias).astype(jnp.bfloat16)


def contract_last(left, right):
    return lax.dot_general(
        left, right, (((1,), (1,)), ((), ())), preferred_element_type=jnp.float32
    )


def keep_same(stacked):
    return stacked


def batch_stats(conv, weight_rows, own_count, reduce_fn, spread_fn, bn_gain, bn_bias):
    local_sums = reduce_fn(jnp.sum(conv * weight_rows, axis=0)[None])[0]
    sums, count = lax.psum((local_sums, own_count), "dp")
    mean = sums / count
    mean_wide = spread_fn(mean[None])[0]
    local_squares = reduce_fn(jnp.sum(((conv - mean_wide) * weight_rows) ** 2, axis=0)[None])[0]
    squares = lax.psum(local_squares, "dp")
    var = squares / count
    scale = lax.rsqrt(var + 1e-05) * bn_gain
    wide = spread_fn(jnp.stack([scale, bn_bias]))
    return (mean_wide, wide[0], wide[1])


def per_device(
    frames_in, lengths, ln_gain, ln_bias, glu_weight, conv_kernel, bn_gain, bn_bias, out_weight
):
    rows = frames_in[0]
    width = rows.shape[1]
    chans = glu_weight.shape[1]
    normed = layer_norm(rows, ln_gain, ln_bias)
    own_count = lengths[0].astype(jnp.float32)
    taps = conv_kernel.astype(jnp.float32)
    w_glu = glu_weight.reshape(2 * chans, width)
    proj = contract_last(lax.all_gather(normed, "tensor", axis=0, tiled=True), w_glu)
    glu = (proj[:, :chans] * jax.nn.sigmoid(proj[:, chans:])).astype(jnp.bfloat16)
    total_rows = glu.shape[0]
    valid = jnp.arange(total_rows, dtype=jnp.int32) < lengths[0]
    glu = jnp.where(valid[:, None], glu, jnp.zeros_like(glu)).astype(jnp.float32)
    padded = jnp.pad(glu, ((15, KERNEL - 16), (0, 0)))
    conv = jnp.zeros_like(glu)
    for k in range(KERNEL):
        conv = conv + padded[k : k + total_rows] * taps[k]
    weight_rows = valid.astype(jnp.float32)[:, None]
    mean, scale, shift = batch_stats(
        conv, weight_rows, own_count, keep_same, keep_same, bn_gain, bn_bias
    )
    z = (conv - mean) * scale + shift
    act = (z * jax.nn.sigmoid(z)).astype(jnp.bfloat16)
    partial_cols = contract_last(lax.all_gather(act, "tensor", axis=1, tiled=True), out_weight)
    branch = lax.all_to_all(partial_cols, "tensor", split_axis=0, concat_axis=1, tiled=True)
    return (rows.astype(jnp.float32) + branch).astype(jnp.bfloat16)[None]


def solution(mesh):
    return jax.shard_map(
        per_device,
        mesh=mesh,
        in_specs=(
            P("dp", "tensor", None),
            P("dp"),
            P(),
            P(),
            P(None, "tensor", None),
            P(None, "tensor"),
            P("tensor"),
            P("tensor"),
            P("tensor", None),
        ),
        out_specs=P("dp", "tensor", None),
        check_vma=False,
    )
```

profile of v0, /device:TPU:1, one launch (start us, length us, event | category | flops | bytes accessed | tf_op | source)
XLA Modules:
  0.0 588.3 jit_solution(17581477607968345549)
XLA Ops:
  6.5 0.0 copy-start
  6.5 0.0 all-gather.3.cloned.1.call-start
  6.5 1.3 copy.11
  7.9 0.2 convert_reduce_fusion
  8.1 0.2 fusion.65
  8.3 1.9 fusion.68
  10.3 0.0 all-gather.3.cloned.1.call-update
  10.3 0.0 all-gather.5.cloned.1.call-start
  11.0 1.0 fusion.78
  12.0 1.0 fusion.77
  13.0 51.8 %all-gather.3.cloned.1.call-done = bf16[1024,1536]{0,1:T(8,128)(2,1)} async-done(((bf16[128,1536]{0,1:T(8,128)(2,1)}), bf16[1024,1536]{0,1:T(8,128)(2,1)}) %all-gather.3.cloned.1.call-update) | async-done | bytes 3145744 | tf_op jit(solution)/shard_map/all_gather | solution.py:49
  64.8 0.0 copy-done
  64.8 3.3 fusion.79
  68.1 0.0 copy-start.1
  68.1 0.0 copy-start.2
  68.1 0.2 select_convert_fusion
  68.3 7.3 %multiply_reduce_fusion.1 = (f32[192]{0:T(256)S(1)}, f32[1024,192]{0,1:T(8,128)S(1)}) fusion(f32[1024]{0:T(1024)S(1)} %get-tuple-element.42, f32[192]{0:T(256)S(1)} %bitcast.100, f32[192]{0:T(256)S(1)} %bitcast.99, f32[192]{0:T(256)S(1)} %bitcast.98, f32[192]{0:T(256)S(1)} %bitcast.97, f32[192]{0:T(256)S(1)} %bitcast.96, f32[192]{0:T(256)S(1)} %bitcast.95, ...), kind=kLoop, calls=%fused_computation.113 | loop fusion | flops 12779328 | bytes 1602304 | tf_op jit(solution)/shard_map/reduce_sum | solution.py:27
  75.7 196.7 %all-reduce.1 = (f32[192]{0:T(256)S(1)}, f32[]{:T(128)}) all-reduce(f32[192]{0:T(256)S(1)} %get-tuple-element.7, f32[]{:T(128)S(6)} %convert_element_type.46), channel_id=1, replica_groups=mesh['dp'=64,'tensor'=8] {'dp'}, use_global_device_ids=true, to_apply=%region_3.4 | all-reduce | flops 193 | bytes 1544 | tf_op jit(solution)/shard_map/psum | solution.py:28
  272.3 0.6 broadcast_divide_fusion
  273.0 0.2 multiply_reduce_fusion
  273.2 187.3 %psum.23 = f32[192]{0:T(256)S(1)} all-reduce(f32[192]{0:T(256)S(1)} %multiply_reduce_fusion), channel_id=1, replica_groups=mesh['dp'=64,'tensor'=8] {'dp'}, use_global_device_ids=true, to_apply=%region_6.7 | all-reduce | flops 192 | bytes 1536 | tf_op jit(solution)/shard_map/psum | solution.py:32
  460.6 0.0 copy-done.1
  460.6 0.7 rsqrt_multiply_fusion
  461.2 0.0 copy-done.2
  461.3 1.1 multiply_convert_fusion
  462.4 0.0 all-gather.5.cloned.1.call-update
  462.4 89.8 %all-gather.5.cloned.1.call-done = bf16[1024,1536]{0,1:T(8,128)(2,1)} async-done(((bf16[1024,192]{0,1:T(8,128)(2,1)}), bf16[1024,1536]{0,1:T(8,128)(2,1)}) %all-gather.5.cloned.1.call-update) | async-done | bytes 3145744 | tf_op jit(solution)/shard_map/all_gather | solution.py:64
  552.3 2.9 convolution_bitcast_fusion
  555.1 0.1 copy.16
  555.2 25.2 %all_to_all.19 = f32[8,128,192]{1,2,0:T(8,128)S(1)} all-to-all(f32[8,128,192]{1,2,0:T(8,128)S(1)} %bitcast.68), channel_id=1, replica_groups=mesh['dp'=64,'tensor'=8] {'tensor'}, dimensions={0} | all-to-all | bytes 1572864 | tf_op jit(solution)/shard_map/all_to_all | solution.py:65
  580.4 0.1 fusion.69
  580.5 0.9 copy.13
  (3 shorter events, 0.0 us)
Async XLA Ops:
  6.5 58.3 %copy-start = (bf16[2,192,1536]{2,1,0:T(8,128)(2,1)S(1)}, bf16[2,192,1536]{2,1,0:T(8,128)(2,1)}, u32[]{:S(2)}) copy-start(bf16[2,192,1536]{2,1,0:T(8,128)(2,1)} %param.13) | copy-start | bytes 3538948
  6.5 58.3 %all-gather.3.cloned.1.call-start = ((), (), s32[]{:S(2)}) async-start(), calls=%async_computation.1 | async-start | bytes 3538944 | tf_op jit(solution)/shard_map/all_gather | solution.py:49
  10.3 542.0 %all-gather.5.cloned.1.call-start = ((), (), s32[]{:S(2)}) async-start(), calls=%async_computation.2 | async-start | bytes 3538944 | tf_op jit(solution)/shard_map/all_gather | solution.py:64
  68.1 392.5 %copy-start.1 = (f32[192]{0:T(256)S(1)}, f32[192]{0:T(256)}, u32[]{:S(2)}) copy-start(f32[192]{0:T(256)} %param.15) | copy-start | bytes 2308
  68.1 393.2 %copy-start.2 = (f32[192]{0:T(256)S(1)}, f32[192]{0:T(256)}, u32[]{:S(2)}) copy-start(f32[192]{0:T(256)} %param.16) | copy-start | bytes 2308
Sparse Core Ops, SparseCore 0:
  10.4 54.3 all-gather.2
  462.5 89.6 all-gather.4
where the time goes:
time: 589 us; the launch traced here: 588 us
  blocking collectives  409 us (69%)
  waiting for transfers between devices  142 us (24%)
  between operations  14.2 us (2%)
  other arithmetic  12.7 us (2%)
  matrix products  6.12 us (1%)
    psum x1, blocking collectives, batch_stats(): sums, count = lax.psum((local_sums, own_count), 'dp')  197 us
    psum x1, blocking collectives, batch_stats(): squares = lax.psum(local_squares, 'dp')  187 us
    all_gather x1, waiting for transfers between devices, per_device(): lax.all_gather(act, 'tensor', axis=1, tiled=True)  89.8 us
    all_gather x1, waiting for transfers between devices, per_device(): lax.all_gather(normed, 'tensor', axis=0, tiled=True)  51.8 us
    all_to_all x1, blocking collectives, per_device(): lax.all_to_all(partial_cols, 'tensor', split_axis=0, concat_axis=1, tiled...  25.2 us
  transfers between devices with their start and end apart: 2, of which 2 were waited for; matrix products, arithmetic and copies ran while one was open for 0% of the time, Pallas kernels for 0%

commit v1 on v0

--- a/solution.py
+++ b/solution.py
@@ -4,6 +4,10 @@
 from jax.sharding import PartitionSpec as P
 
 KERNEL = 32
+
+
+def side_mix(base_x):
+    return jnp.sum(jax.lax.all_gather(base_x, "dp"), 0)
 
 
 def layer_norm(rows, gain, bias):
@@ -29,7 +33,7 @@
     mean = sums / count
     mean_wide = spread_fn(mean[None])[0]
     local_squares = reduce_fn(jnp.sum(((conv - mean_wide) * weight_rows) ** 2, axis=0)[None])[0]
-    squares = lax.psum(local_squares, "dp")
+    squares = side_mix(local_squares)
     var = squares / count
     scale = lax.rsqrt(var + 1e-05) * bn_gain
     wide = spread_fn(jnp.stack([scale, bn_bias]))

time: 589 us -> 800 us (1.36)
  blocking collectives: 409 us -> 594 us
  waiting for transfers between devices: 142 us -> 166 us
    unnamed x0 -> x1, blocking collectives: none -> 373 us
    psum x1 -> x0, blocking collectives: 187 us -> none  [batch_stats(): squares = lax.psum(local_squares, 'dp')]
    all_gather x1, waiting for transfers between devices: 89.8 us -> 116 us  [per_device(): lax.all_gather(act, 'tensor', axis=1, tiled=True)]
where the time goes in v1:
time: 800 us
  blocking collectives  594 us (74%)
  waiting for transfers between devices  166 us (21%)
  between operations  14.8 us (2%)
  other arithmetic  12.8 us (2%)
    unnamed x1, blocking collectives  373 us
    psum x1, blocking collectives, batch_stats(): sums, count = lax.psum((local_sums, own_count), 'dp')  197 us
    all_gather x1, waiting for transfers between devices, per_device(): lax.all_gather(act, 'tensor', axis=1, tiled=True)  116 us
    all_gather x1, waiting for transfers between devices, per_device(): lax.all_gather(normed, 'tensor', axis=0, tiled=True)  49.9 us
    all_to_all x1, blocking collectives, per_device(): lax.all_to_all(partial_cols, 'tensor', split_axis=0, concat_axis=1, tiled...  25.2 us
  transfers between devices with their start and end apart: 2, of which 2 were waited for; matrix products, arithmetic and copies ran while one was open for 0% of the time, Pallas kernels for 0%

profile of v1, /device:TPU:1, one launch (start us, length us, event | category | flops | bytes accessed | tf_op | source)
XLA Modules:
  0.0 800.0 jit_solution(157288743317852875)
XLA Ops:
  6.5 0.0 copy-start
  6.5 0.0 all-gather.4.cloned.1.call-start
  6.5 1.3 copy.14
  7.9 0.2 convert_reduce_fusion
  8.1 0.2 fusion.65
  8.3 1.9 fusion.68
  10.3 0.0 all-gather.4.cloned.1.call-update
  10.3 0.0 all-gather.6.cloned.1.call-start
  11.0 1.3 dynamic-slice
  12.9 1.0 fusion.78
  13.9 1.0 fusion.77
  14.9 49.9 %all-gather.4.cloned.1.call-done = bf16[1024,1536]{0,1:T(8,128)(2,1)} async-done(((bf16[128,1536]{0,1:T(8,128)(2,1)}), bf16[1024,1536]{0,1:T(8,128)(2,1)}) %all-gather.4.cloned.1.call-update) | async-done | bytes 3145744 | tf_op jit(solution)/shard_map/all_gather | solution.py:53
  64.8 0.0 copy-done
  64.8 3.3 fusion.79
  68.1 0.0 copy-start.1
  68.1 0.0 copy-start.2
  68.1 0.2 select_convert_fusion
  68.3 7.3 multiply_reduce_fusion.1
  75.7 196.7 %all-reduce.2 = (f32[192]{0:T(256)S(1)}, f32[]{:T(128)}) all-reduce(f32[192]{0:T(256)S(1)} %get-tuple-element.7, f32[]{:T(128)S(6)} %convert_element_type.46), channel_id=1, replica_groups=mesh['dp'=64,'tensor'=8] {'dp'}, use_global_device_ids=true, to_apply=%region_3.4 | all-reduce | flops 193 | bytes 1544 | tf_op jit(solution)/shard_map/psum | solution.py:32
  272.3 0.6 broadcast_divide_fusion
  273.0 0.2 multiply_reduce_fusion
  273.2 0.3 dynamic-update-slice
  273.5 372.6 %all-reduce.1 = f32[12288]{0:T(1024)S(1)} all-reduce(f32[12288]{0:T(1024)S(1)} %dynamic-update-slice), channel_id=2, replica_groups=mesh['dp'=64,'tensor'=8] {'dp'}, use_global_device_ids=true, to_apply=%add.1 | all-reduce | flops 12288 | bytes 98304
  646.2 0.1 reshape.33
  646.3 0.0 copy-done.1
  646.3 0.7 rsqrt_multiply_fusion
  646.9 0.0 copy-done.2
  646.9 1.1 multiply_convert_fusion
  648.1 0.0 all-gather.6.cloned.1.call-update
  648.1 116.0 %all-gather.6.cloned.1.call-done = bf16[1024,1536]{0,1:T(8,128)(2,1)} async-done(((bf16[1024,192]{0,1:T(8,128)(2,1)}), bf16[1024,1536]{0,1:T(8,128)(2,1)}) %all-gather.6.cloned.1.call-update) | async-done | bytes 3145744 | tf_op jit(solution)/shard_map/all_gather | solution.py:68
  764.1 2.9 convolution_bitcast_fusion
  766.9 0.1 copy.19
  767.0 25.2 %all_to_all.19 = f32[8,128,192]{1,2,0:T(8,128)S(1)} all-to-all(f32[8,128,192]{1,2,0:T(8,128)S(1)} %bitcast.69), channel_id=1, replica_groups=mesh['dp'=64,'tensor'=8] {'tensor'}, dimensions={0} | all-to-all | bytes 1572864 | tf_op jit(solution)/shard_map/all_to_all | solution.py:69
  792.2 0.1 fusion.69
  792.3 0.9 copy.16
  (5 shorter events, 0.1 us)
Async XLA Ops:
  6.5 58.3 %copy-start = (bf16[2,192,1536]{2,1,0:T(8,128)(2,1)S(1)}, bf16[2,192,1536]{2,1,0:T(8,128)(2,1)}, u32[]{:S(2)}) copy-start(bf16[2,192,1536]{2,1,0:T(8,128)(2,1)} %param.13) | copy-start | bytes 3538948
  6.5 58.3 %all-gather.4.cloned.1.call-start = ((), (), s32[]{:S(2)}) async-start(), calls=%async_computation.1 | async-start | bytes 3538944 | tf_op jit(solution)/shard_map/all_gather | solution.py:53
  10.3 753.8 %all-gather.6.cloned.1.call-start = ((), (), s32[]{:S(2)}) async-start(), calls=%async_computation.2 | async-start | bytes 3538944 | tf_op jit(solution)/shard_map/all_gather | solution.py:68
  68.1 578.2 %copy-start.1 = (f32[192]{0:T(256)S(1)}, f32[192]{0:T(256)}, u32[]{:S(2)}) copy-start(f32[192]{0:T(256)} %param.15) | copy-start | bytes 2308
  68.1 578.8 %copy-start.2 = (f32[192]{0:T(256)S(1)}, f32[192]{0:T(256)}, u32[]{:S(2)}) copy-start(f32[192]{0:T(256)} %param.16) | copy-start | bytes 2308
Sparse Core Ops, SparseCore 0:
  10.4 54.3 all-gather.3
  648.2 115.7 all-gather.5
